TPU v7x, 512 devices: a whole 4x8x8 slice. The times are simulated.
512 devices in a mesh: cluster: 16 (over z, x_lo), sub: 32 (over y, x_hi, core).
Axes of the slice: x: 4 (x_hi: 2, x_lo: 2; x = x_hi * 2 + x_lo), y: 8, z: 8, core: 2. Of those that a mesh axis runs over, the one named last changes fastest.
Arguments:
- schur_block: bfloat16 [16, 32, 1024, 1024], P('cluster', 'sub'), as said below
- load_cases: float32 [16, 32, 1024, 64], P('cluster', 'sub'), may hold values from -30 to 30
- precond_scale: float32 [16, 32, 1024], P('cluster', 'sub'), may hold values from 0.5 to 2
- coarse_basis: float32 [16, 32, 6, 1024], P('cluster', 'sub'), may hold values from -1 to 1
- coarse_inverse: float32 [16, 192, 192], P('cluster', 'sub'), as said below
- corner_weight: float32 [16, 512], P('cluster', 'sub'), may hold values from 0.5 to 4
- corner_index: int32 [16, 32, 64], P('cluster', 'sub'), may hold values from 0 to 511
- iface_block: int32 [16, 32, 2], P('cluster', 'sub'), may hold values from 0 to 6
- glue_link: int32 [16, 32], P('cluster', 'sub'), may hold values 0 or 1
Outputs:
- solution: float32 [16, 32, 1024, 64], P('cluster', 'sub')
Inputs may be any that keep to these rules, and one draw needn't show every extreme that they name: `schur_block`: each block is symmetric positive definite. `coarse_inverse`: each cluster's matrix is symmetric positive definite.
All inputs are finite; a program needn't handle non-finite values. No bound on the sum of `glue_link` on one device may be relied on, other than what follows from the above.
Results may differ from a plain program's by a relative error of at most 0.0007.
Values sent between devices are 32-bit elements; how exact they have to be, the bound alone decides.
A program may use at most 64 MiB of HBM per device.

v0:
```python
import jax
import jax.numpy as jnp
from jax import lax
from jax.sharding import PartitionSpec as P

NC = 64
NI = 128
ITERS = 3
highest = lax.Precision.HIGHEST


def shifted(block, axis, distance):
    devices = range(lax.axis_size(axis))
    route = [((i - distance) % len(devices), i) for i in devices]
    return lax.ppermute(block, axis, route)


def inner(first_vec, second_vec):
    return jnp.sum(first_vec * second_vec, axis=0)


def per_device(
    schur_block,
    load_cases,
    precond_scale,
    coarse_basis,
    coarse_inverse,
    corner_weight,
    corner_index,
    iface_block,
    glue_link,
):
    matrix = schur_block[0, 0]
    loads_here = load_cases[0, 0]
    weights = precond_scale[0, 0][:, None]
    basis_rows = coarse_basis[0, 0]
    inverse_rows = coarse_inverse[0]
    owner_gains = corner_weight[0]
    corners = corner_index[0, 0]
    blocks = iface_block[0, 0]
    glue_flag = glue_link[0].astype(jnp.float32)
    owned_count = owner_gains.shape[0]
    corner_total = owned_count * lax.axis_size("sub")
    selector = (corners[:, None] == jnp.arange(corner_total, dtype=jnp.int32)[None, :]).astype(
        jnp.float32
    )
    left_row = NC + blocks[0] * NI
    right_row = NC + blocks[1] * NI

    def precondition(vector):
        pieces = jnp.dot(basis_rows, vector, precision=highest, preferred_element_type=jnp.float32)
        gathered = lax.all_gather(pieces, "sub", axis=0, tiled=True)
        coarse = jnp.dot(
            inverse_rows, gathered, precision=highest, preferred_element_type=jnp.float32
        )
        return weights * vector + jnp.einsum(
            "nw,nr->wr", basis_rows, coarse, precision=highest, preferred_element_type=jnp.float32
        )

    solution = jnp.zeros_like(loads_here)
    residual = loads_here
    precond = precondition(residual)
    direction = precond
    rho_now = lax.psum(inner(residual, precond), ("cluster", "sub"))
    for iteration in range(ITERS):
        applied = jnp.dot(
            matrix, direction.astype(jnp.bfloat16), preferred_element_type=jnp.float32
        )
        corner_rows = direction[:NC]
        owned = lax.psum_scatter(
            jnp.einsum(
                "jk,jr->kr",
                selector,
                corner_rows,
                precision=highest,
                preferred_element_type=jnp.float32,
            ),
            "sub",
            scatter_dimension=0,
            tiled=True,
        )
        scaled = owned * owner_gains[:, None]
        back = jnp.einsum(
            "jk,kr->jr",
            selector,
            lax.all_gather(scaled, "sub", axis=0, tiled=True),
            precision=highest,
            preferred_element_type=jnp.float32,
        )
        applied = jnp.concatenate([applied[:NC] + back, applied[NC:]], axis=0)
        left_block = lax.dynamic_slice_in_dim(direction, left_row, NI, 0)
        right_block = lax.dynamic_slice_in_dim(direction, right_row, NI, 0)
        prev_right, prev_glue = shifted((right_block, glue_flag), "cluster", 1)
        next_left = shifted(left_block, "cluster", -1)
        jump_right = glue_flag[0] * (right_block - next_left)
        jump_left = prev_glue[0] * (prev_right - left_block)
        applied = lax.dynamic_update_slice_in_dim(
            applied, lax.dynamic_slice_in_dim(applied, right_row, NI, 0) + jump_right, right_row, 0
        )
        applied = lax.dynamic_update_slice_in_dim(
            applied, lax.dynamic_slice_in_dim(applied, left_row, NI, 0) - jump_left, left_row, 0
        )
        curve = lax.psum(inner(direction, applied), ("cluster", "sub"))
        step_size = rho_now / curve
        solution = solution + step_size * direction
        if iteration + 1 < ITERS:
            residual = residual - step_size * applied
            precond = precondition(residual)
            rho_next = lax.psum(inner(residual, precond), ("cluster", "sub"))
            direction = precond + rho_next / rho_now * direction
            rho_now = rho_next
    return solution[None, None]


def solution(mesh):
    in_specs = (
        P("cluster", "sub", None, None),
        P("cluster", "sub", None, None),
        P("cluster", "sub", None),
        P("cluster", "sub", None, None),
        P("cluster", "sub", None),
        P("cluster", "sub"),
        P("cluster", "sub", None),
        P("cluster", "sub", None),
        P("cluster", "sub"),
    )
    out_specs = P("cluster", "sub", None, None)
    return jax.shard_map(
        per_device, mesh=mesh, in_specs=in_specs, out_specs=out_specs, check_vma=False
    )
```

profile of v0, /device:TPU:1, one launch (start us, length us, event | category | flops | bytes accessed | tf_op | source)
XLA Modules:
  0.0 1135.0 jit_solution(11785621884392652291)
XLA Ops:
  7.9 44.0 %all-gather = f32[32,6,64]{2,1,0:T(8,128)S(1)} all-gather(f32[1,6,64]{2,1,0:T(8,128)S(1)} %convolution_bitcast_fusion.5), channel_id=1, replica_groups=mesh['cluster'=16,'sub'=32] {'sub'}, dimensions={0}, use_global_device_ids=true | all-gather | bytes 50688 | tf_op jit(solution)/shard_map/all_gather | solution.py:52
  58.2 10.7 collective-permute-start
  69.5 2.6 collective-permute-start.1
  73.7 99.0 %reduce-scatter.4.cloned.1.call-done = f32[16,64]{1,0:T(8,128)} async-done(((f32[512,64]{1,0:T(8,128)}), f32[16,64]{1,0:T(8,128)}) %reduce-scatter.4.cloned.1.call-update) | async-done | bytes 4112 | tf_op jit(solution)/shard_map/reduce_scatter | solution.py:70
  173.5 45.6 %all_gather.19 = f32[512,64]{1,0:T(8,128)S(1)} all-gather(f32[16,64]{1,0:T(8,128)S(1)} %broadcast_multiply_fusion.2), channel_id=1, replica_groups=mesh['cluster'=16,'sub'=32] {'sub'}, dimensions={0}, use_global_device_ids=true | all-gather | bytes 135168 | tf_op jit(solution)/shard_map/all_gather | solution.py:86
  219.7 2.2 collective-permute-start.2
  222.6 4.0 collective-permute-done.2
  228.0 95.8 %all-reduce = (f32[64]{0:T(128)S(1)}, f32[64]{0:T(128)S(1)}) all-reduce(f32[64]{0:T(128)S(1)} %get-tuple-element.6, f32[64]{0:T(128)S(1)} %get-tuple-element.5), channel_id=1, replica_groups=mesh['cluster'=16,'sub'=32] {'cluster','sub'}, use_global_device_ids=true, to_apply=%region_1.0 | all-reduce | flops 128 | bytes 1024 | tf_op jit(solution)/shard_map/psum | solution.py:64
  324.3 39.2 %all-gather.1 = f32[32,6,64]{2,1,0:T(8,128)S(1)} all-gather(f32[1,6,64]{2,1,0:T(8,128)S(1)} %convolution_bitcast_fusion.4), channel_id=1, replica_groups=mesh['cluster'=16,'sub'=32] {'sub'}, dimensions={0}, use_global_device_ids=true | all-gather | bytes 50688 | tf_op jit(solution)/shard_map/all_gather | solution.py:52
  364.2 95.5 %psum.44 = f32[64]{0:T(128)S(1)} all-reduce(f32[64]{0:T(128)S(1)} %get-tuple-element.17), channel_id=1, replica_groups=mesh['cluster'=16,'sub'=32] {'cluster','sub'}, use_global_device_ids=true, to_apply=%region_6.0 | all-reduce | flops 64 | bytes 512 | tf_op jit(solution)/shard_map/psum | solution.py:109
  462.0 3.5 collective-permute-start.3
  465.5 108.9 %reduce-scatter.6.cloned.1.call-done = f32[16,64]{1,0:T(8,128)} async-done(((f32[512,64]{1,0:T(8,128)}), f32[16,64]{1,0:T(8,128)}) %reduce-scatter.6.cloned.1.call-update) | async-done | bytes 4112 | tf_op jit(solution)/shard_map/reduce_scatter | solution.py:70
  575.1 45.4 %all_gather.21 = f32[512,64]{1,0:T(8,128)S(1)} all-gather(f32[16,64]{1,0:T(8,128)S(1)} %broadcast_multiply_fusion.1), channel_id=1, replica_groups=mesh['cluster'=16,'sub'=32] {'sub'}, dimensions={0}, use_global_device_ids=true | all-gather | bytes 135168 | tf_op jit(solution)/shard_map/all_gather | solution.py:86
  621.6 2.3 collective-permute-start.4
  624.6 4.2 collective-permute-done.4
  630.3 95.8 %psum.45 = f32[64]{0:T(128)S(1)} all-reduce(f32[64]{0:T(128)S(1)} %multiply_reduce_fusion.2), channel_id=1, replica_groups=mesh['cluster'=16,'sub'=32] {'cluster','sub'}, use_global_device_ids=true, to_apply=%region_9.0 | all-reduce | flops 64 | bytes 512 | tf_op jit(solution)/shard_map/psum | solution.py:103
  726.5 39.1 %all-gather.2 = f32[32,6,64]{2,1,0:T(8,128)S(1)} all-gather(f32[1,6,64]{2,1,0:T(8,128)S(1)} %convolution_bitcast_fusion.3), channel_id=1, replica_groups=mesh['cluster'=16,'sub'=32] {'sub'}, dimensions={0}, use_global_device_ids=true | all-gather | bytes 50688 | tf_op jit(solution)/shard_map/all_gather | solution.py:52
  766.4 95.7 %psum.46 = f32[64]{0:T(128)S(1)} all-reduce(f32[64]{0:T(128)S(1)} %get-tuple-element.19), channel_id=1, replica_groups=mesh['cluster'=16,'sub'=32] {'cluster','sub'}, use_global_device_ids=true, to_apply=%region_11.0 | all-reduce | flops 64 | bytes 512 | tf_op jit(solution)/shard_map/psum | solution.py:109
  864.3 3.4 collective-permute-start.5
  867.7 108.9 %reduce-scatter.8.cloned.1.call-done = f32[16,64]{1,0:T(8,128)} async-done(((f32[512,64]{1,0:T(8,128)}), f32[16,64]{1,0:T(8,128)}) %reduce-scatter.8.cloned.1.call-update) | async-done | bytes 4112 | tf_op jit(solution)/shard_map/reduce_scatter | solution.py:70
  977.4 45.5 %all_gather.23 = f32[512,64]{1,0:T(8,128)S(1)} all-gather(f32[16,64]{1,0:T(8,128)S(1)} %broadcast_multiply_fusion), channel_id=1, replica_groups=mesh['cluster'=16,'sub'=32] {'sub'}, dimensions={0}, use_global_device_ids=true | all-gather | bytes 135168 | tf_op jit(solution)/shard_map/all_gather | solution.py:86
  1023.4 2.2 collective-permute-start.6
  1026.3 3.9 collective-permute-done.6
  1031.7 95.9 %psum.47 = f32[64]{0:T(128)S(1)} all-reduce(f32[64]{0:T(128)S(1)} %multiply_reduce_fusion), channel_id=1, replica_groups=mesh['cluster'=16,'sub'=32] {'cluster','sub'}, use_global_device_ids=true, to_apply=%region_14.0 | all-reduce | flops 64 | bytes 512 | tf_op jit(solution)/shard_map/psum | solution.py:103
  (83 shorter events, 26.3 us)
Async XLA Ops:
  6.5 66.2 %copy-start = (bf16[1,1,1024,1024]{3,2,1,0:T(8,128)(2,1)S(1)}, bf16[1,1,1024,1024]{3,2,1,0:T(8,128)(2,1)}, u32[]{:S(2)}) copy-start(bf16[1,1,1024,1024]{3,2,1,0:T(8,128)(2,1)} %param.9) | copy-start | bytes 6291460
  6.5 166.2 %reduce-scatter.4.cloned.1.call-start = ((), (), s32[]{:S(2)}) async-start(), calls=%async_computation.3 | async-start | bytes 270336 | tf_op jit(solution)/shard_map/reduce_scatter | solution.py:70
  52.8 119.9 %copy-start.6 = (f32[1,16]{1,0:T(1,128)S(1)}, f32[1,16]{1,0:T(1,128)}, u32[]{:S(2)}) copy-start(f32[1,16]{1,0:T(1,128)} %param.14) | copy-start | bytes 196
  54.2 164.9 %copy-start.5 = (s32[1,1,64]{2,1,0:T(1,128)S(1)}, s32[1,1,64]{2,1,0:T(1,128)}, u32[]{:S(2)}) copy-start(s32[1,1,64]{2,1,0:T(1,128)} %param.15) | copy-start | bytes 772
  56.1 518.3 %reduce-scatter.6.cloned.1.call-start = ((), (), s32[]{:S(2)}) async-start(), calls=%async_computation.4 | async-start | bytes 270336 | tf_op jit(solution)/shard_map/reduce_scatter | solution.py:70
  58.2 161.4 %collective-permute-start = (f32[128,64]{0,1:T(8,128)S(1)}, f32[128,64]{0,1:T(8,128)S(1)}, u32[]{:S(2)}, u32[]{:S(2)}) collective-permute-start(f32[128,64]{0,1:T(8,128)S(1)} %constant_dynamic-slice_fusion.4), channel_id=1, source_target_pairs={{32,0},{64,32},{96,64},{128,96},{160,128},{192,160},{224,192},{256... | collective-permute-start | bytes 98312 | tf_op jit(solution)/shard_map/ppermute | solution.py:15
  69.5 153.1 %collective-permute-start.1 = (f32[1]{0:T(128)}, f32[1]{0:T(128)}, u32[]{:S(2)}, u32[]{:S(2)}) collective-permute-start(f32[1]{0:T(128)} %bitcast.13), channel_id=1, source_target_pairs={{480,0},{0,32},{32,64},{64,96},{96,128},{128,160},{160,192},{192,2... | collective-permute-start | bytes 20 | tf_op jit(solution)/shard_map/ppermute | solution.py:15
  72.8 155.1 %copy-start.1 = (f32[1,1,1024,64]{2,3,1,0:T(8,128)S(1)}, f32[1,1,1024,64]{2,3,1,0:T(8,128)}, u32[]{:S(2)}) copy-start(f32[1,1,1024,64]{2,3,1,0:T(8,128)} %param.10) | copy-start | bytes 786436
  73.5 250.4 %copy-start.2 = (f32[1,1,6,1024]{3,1,2,0:T(1,128)S(1)}, f32[1,1,6,1024]{3,1,2,0:T(1,128)}, u32[]{:S(2)}) copy-start(f32[1,1,6,1024]{3,1,2,0:T(1,128)} %param.12) | copy-start | bytes 73732
  73.7 289.8 %copy-start.3 = (f32[1,6,192]{2,0,1:T(1,128)S(1)}, f32[1,6,192]{2,0,1:T(1,128)}, u32[]{:S(2)}) copy-start(f32[1,6,192]{2,0,1:T(1,128)} %param.13) | copy-start | bytes 13828
  173.5 190.2 %copy-start.4 = (f32[1,1,1024]{2,1,0:T(1,128)S(1)}, f32[1,1,1024]{2,1,0:T(1,128)}, u32[]{:S(2)}) copy-start(f32[1,1,1024]{2,1,0:T(1,128)} %param.11) | copy-start | bytes 12292
  219.7 6.9 collective-permute-start.2
  460.9 515.7 %reduce-scatter.8.cloned.1.call-start = ((), (), s32[]{:S(2)}) async-start(), calls=%async_computation.5 | async-start | bytes 270336 | tf_op jit(solution)/shard_map/reduce_scatter | solution.py:70
  462.0 158.9 %collective-permute-start.3 = (f32[128,64]{0,1:T(8,128)S(1)}, f32[128,64]{0,1:T(8,128)S(1)}, u32[]{:S(2)}, u32[]{:S(2)}) collective-permute-start(f32[128,64]{0,1:T(8,128)S(1)} %constant_dynamic-slice_fusion.2), channel_id=1, source_target_pairs={{32,0},{64,32},{96,64},{128,96},{160,128},{192,160},{224,192},{256... | collective-permute-start | bytes 98312 | tf_op jit(solution)/shard_map/ppermute | solution.py:15
  621.6 7.2 collective-permute-start.4
  864.3 159.0 %collective-permute-start.5 = (f32[128,64]{0,1:T(8,128)S(1)}, f32[128,64]{0,1:T(8,128)S(1)}, u32[]{:S(2)}, u32[]{:S(2)}) collective-permute-start(f32[128,64]{0,1:T(8,128)S(1)} %constant_dynamic-slice_fusion), channel_id=1, source_target_pairs={{32,0},{64,32},{96,64},{128,96},{160,128},{192,160},{224,192},{256... | collective-permute-start | bytes 98312 | tf_op jit(solution)/shard_map/ppermute | solution.py:15
  1023.4 6.9 collective-permute-start.6
Sparse Core Ops, SparseCore 0:
  56.2 116.4 reduce-scatter.3
  461.1 113.2 reduce-scatter.5
  863.4 113.1 reduce-scatter.7
where the time goes:
time: 1140 us; the launch traced here: 1130 us
  blocking collectives  738 us (65%)
  waiting for transfers between devices  329 us (29%)
  starting transfers between devices  27 us (2%)
  between operations  15.3 us (1%)
  matrix products  13.1 us (1%)
    reduce_scatter x3, waiting for transfers between devices, per_device(): lax.psum_scatter(jnp.einsum('jk,jr->kr', selector, corner_rows, precision...  317 us
    psum x2, blocking collectives, per_device(): curve = lax.psum(inner(direction, applied), ('cluster', 'sub'))  192 us
    psum x2, blocking collectives, per_device(): rho_next = lax.psum(inner(residual, precond), ('cluster', 'sub'))  191 us
    all_gather x3, blocking collectives, per_device(): lax.all_gather(scaled, 'sub', axis=0, tiled=True)  136 us
    all_gather x3, blocking collectives, precondition(): gathered = lax.all_gather(pieces, 'sub', axis=0, tiled=True)  122 us
    psum x1, blocking collectives, per_device(): rho_now = lax.psum(inner(residual, precond), ('cluster', 'sub'))  95.8 us
    ppermute x7, starting transfers between devices, shifted(): return lax.ppermute(block, axis, route)  26.9 us
  transfers between devices with their start and end apart: 10, of which 6 were waited for; matrix products, arithmetic and copies ran while one was open for 1% of the time, Pallas kernels for 0%

commit v1 on v0

--- a/solution.py
+++ b/solution.py
@@ -100,7 +100,7 @@
         applied = lax.dynamic_update_slice_in_dim(
             applied, lax.dynamic_slice_in_dim(applied, left_row, NI, 0) - jump_left, left_row, 0
         )
-        curve = lax.psum(inner(direction, applied), ("cluster", "sub"))
+        curve = jnp.sum(lax.all_gather(inner(direction, applied), ("cluster", "sub")), axis=0)
         step_size = rho_now / curve
         solution = solution + step_size * direction
         if iteration + 1 < ITERS:

time: 1140 us -> 1640 us (1.44)
  waiting for transfers between devices: 329 us -> 1020 us
  blocking collectives: 738 us -> 544 us
    unnamed x3 -> x9, waiting for transfers between devices: 0.05 us -> 697 us
    psum x2 -> x0, blocking collectives: 192 us -> none  [per_device(): curve = lax.psum(inner(direction, applied), ('cluster', 'sub'))]
  transfers between devices with their start and end apart: 10 -> 13, of which waited for: 6 -> 9; matrix products, arithmetic and copies ran while one was open for 1% -> 1% of each run, Pallas kernels for 0% -> 0%
where the time goes in v1:
time: 1640 us
  waiting for transfers between devices  1020 us (62%)
  blocking collectives  544 us (33%)
  starting transfers between devices  28.8 us (2%)
    unnamed x9, waiting for transfers between devices  697 us
    reduce_scatter x3, waiting for transfers between devices, per_device(): lax.psum_scatter(jnp.einsum('jk,jr->kr', selector, corner_rows, precision...  313 us
    psum x2, blocking collectives, per_device(): rho_next = lax.psum(inner(residual, precond), ('cluster', 'sub'))  188 us
    all_gather x3, blocking collectives, per_device(): lax.all_gather(scaled, 'sub', axis=0, tiled=True)  137 us
    all_gather x3, blocking collectives, precondition(): gathered = lax.all_gather(pieces, 'sub', axis=0, tiled=True)  122 us
    psum x1, blocking collectives, per_device(): rho_now = lax.psum(inner(residual, precond), ('cluster', 'sub'))  96.7 us
  transfers between devices with their start and end apart: 13, of which 9 were waited for; matrix products, arithmetic and copies ran while one was open for 1% of the time, Pallas kernels for 0%

profile of v1, /device:TPU:1, one launch (start us, length us, event | category | flops | bytes accessed | tf_op | source)
XLA Modules:
  0.0 1643.8 jit_solution(8904110884188283523)
XLA Ops:
  7.9 44.0 %all-gather.3 = f32[32,6,64]{2,1,0:T(8,128)S(1)} all-gather(f32[1,6,64]{2,1,0:T(8,128)S(1)} %convolution_bitcast_fusion.5), channel_id=1, replica_groups=mesh['cluster'=16,'sub'=32] {'sub'}, dimensions={0}, use_global_device_ids=true | all-gather | bytes 50688 | tf_op jit(solution)/shard_map/all_gather | solution.py:52
  58.2 10.7 collective-permute-start
  69.5 2.6 collective-permute-start.1
  73.6 99.1 %reduce-scatter.4.cloned.1.call-done = f32[16,64]{1,0:T(8,128)} async-done(((f32[512,64]{1,0:T(8,128)}), f32[16,64]{1,0:T(8,128)}) %reduce-scatter.4.cloned.1.call-update) | async-done | bytes 4112 | tf_op jit(solution)/shard_map/reduce_scatter | solution.py:70
  173.5 45.5 %all_gather.37 = f32[512,64]{1,0:T(8,128)S(1)} all-gather(f32[16,64]{1,0:T(8,128)S(1)} %broadcast_multiply_fusion.2), channel_id=1, replica_groups=mesh['cluster'=16,'sub'=32] {'sub'}, dimensions={0}, use_global_device_ids=true | all-gather | bytes 135168 | tf_op jit(solution)/shard_map/all_gather | solution.py:86
  219.5 2.2 collective-permute-start.2
  222.5 4.0 collective-permute-done.2
  229.0 96.7 %psum.21 = f32[64]{0:T(128)S(1)} all-reduce(f32[64]{0:T(128)S(1)} %get-tuple-element.6), channel_id=1, replica_groups=mesh['cluster'=16,'sub'=32] {'cluster','sub'}, use_global_device_ids=true, to_apply=%region_1.0 | all-reduce | flops 64 | bytes 512 | tf_op jit(solution)/shard_map/psum | solution.py:64
  325.7 167.9 %all-reduce.7.cloned.1.call-done = f32[32768]{0:T(1024)} async-done(((f32[32768]{0:T(1024)}), f32[32768]{0:T(1024)}) %all-reduce.7.cloned.1.call-update) | async-done | bytes 131088
  495.0 39.2 %all-gather.4 = f32[32,6,64]{2,1,0:T(8,128)S(1)} all-gather(f32[1,6,64]{2,1,0:T(8,128)S(1)} %convolution_bitcast_fusion.4), channel_id=1, replica_groups=mesh['cluster'=16,'sub'=32] {'sub'}, dimensions={0}, use_global_device_ids=true | all-gather | bytes 50688 | tf_op jit(solution)/shard_map/all_gather | solution.py:52
  534.9 94.2 %psum.22 = f32[64]{0:T(128)S(1)} all-reduce(f32[64]{0:T(128)S(1)} %get-tuple-element.15), channel_id=1, replica_groups=mesh['cluster'=16,'sub'=32] {'cluster','sub'}, use_global_device_ids=true, to_apply=%region_6.0 | all-reduce | flops 64 | bytes 512 | tf_op jit(solution)/shard_map/psum | solution.py:109
  632.0 4.3 collective-permute-start.3
  636.3 107.3 %reduce-scatter.6.cloned.1.call-done = f32[16,64]{1,0:T(8,128)} async-done(((f32[512,64]{1,0:T(8,128)}), f32[16,64]{1,0:T(8,128)}) %reduce-scatter.6.cloned.1.call-update) | async-done | bytes 4112 | tf_op jit(solution)/shard_map/reduce_scatter | solution.py:70
  744.3 45.4 %all_gather.41 = f32[512,64]{1,0:T(8,128)S(1)} all-gather(f32[16,64]{1,0:T(8,128)S(1)} %broadcast_multiply_fusion.1), channel_id=1, replica_groups=mesh['cluster'=16,'sub'=32] {'sub'}, dimensions={0}, use_global_device_ids=true | all-gather | bytes 135168 | tf_op jit(solution)/shard_map/all_gather | solution.py:86
  790.3 2.2 collective-permute-start.4
  793.2 3.9 collective-permute-done.4
  799.7 264.2 %all-reduce.9.cloned.1.call-done = f32[32768]{0:T(1024)} async-done(((f32[32768]{0:T(1024)}), f32[32768]{0:T(1024)}) %all-reduce.9.cloned.1.call-update) | async-done | bytes 131088
  1066.0 39.2 %all-gather.5 = f32[32,6,64]{2,1,0:T(8,128)S(1)} all-gather(f32[1,6,64]{2,1,0:T(8,128)S(1)} %convolution_bitcast_fusion.3), channel_id=1, replica_groups=mesh['cluster'=16,'sub'=32] {'sub'}, dimensions={0}, use_global_device_ids=true | all-gather | bytes 50688 | tf_op jit(solution)/shard_map/all_gather | solution.py:52
  1105.9 94.2 %psum.23 = f32[64]{0:T(128)S(1)} all-reduce(f32[64]{0:T(128)S(1)} %get-tuple-element.17), channel_id=1, replica_groups=mesh['cluster'=16,'sub'=32] {'cluster','sub'}, use_global_device_ids=true, to_apply=%region_11.0 | all-reduce | flops 64 | bytes 512 | tf_op jit(solution)/shard_map/psum | solution.py:109
  1203.3 4.3 collective-permute-start.5
  1207.5 106.8 %reduce-scatter.8.cloned.1.call-done = f32[16,64]{1,0:T(8,128)} async-done(((f32[512,64]{1,0:T(8,128)}), f32[16,64]{1,0:T(8,128)}) %reduce-scatter.8.cloned.1.call-update) | async-done | bytes 4112 | tf_op jit(solution)/shard_map/reduce_scatter | solution.py:70
  1315.1 45.8 %all_gather.45 = f32[512,64]{1,0:T(8,128)S(1)} all-gather(f32[16,64]{1,0:T(8,128)S(1)} %broadcast_multiply_fusion), channel_id=1, replica_groups=mesh['cluster'=16,'sub'=32] {'sub'}, dimensions={0}, use_global_device_ids=true | all-gather | bytes 135168 | tf_op jit(solution)/shard_map/all_gather | solution.py:86
  1364.2 4.0 collective-permute-done.6
  1370.7 264.3 %all-reduce.11.cloned.1.call-done = f32[32768]{0:T(1024)} async-done(((f32[32768]{0:T(1024)}), f32[32768]{0:T(1024)}) %all-reduce.11.cloned.1.call-update) | async-done | bytes 131088
  (110 shorter events, 36.2 us)
Async XLA Ops:
  6.5 66.2 %copy-start = (bf16[1,1,1024,1024]{3,2,1,0:T(8,128)(2,1)S(1)}, bf16[1,1,1024,1024]{3,2,1,0:T(8,128)(2,1)}, u32[]{:S(2)}) copy-start(bf16[1,1,1024,1024]{3,2,1,0:T(8,128)(2,1)} %param.9) | copy-start | bytes 6291460
  6.5 166.2 %reduce-scatter.4.cloned.1.call-start = ((), (), s32[]{:S(2)}) async-start(), calls=%async_computation.3 | async-start | bytes 270336 | tf_op jit(solution)/shard_map/reduce_scatter | solution.py:70
  52.8 119.9 %copy-start.9 = (f32[1,16]{1,0:T(1,128)S(1)}, f32[1,16]{1,0:T(1,128)}, u32[]{:S(2)}) copy-start(f32[1,16]{1,0:T(1,128)} %param.14) | copy-start | bytes 196
  54.2 164.8 %copy-start.8 = (s32[1,1,64]{2,1,0:T(1,128)S(1)}, s32[1,1,64]{2,1,0:T(1,128)}, u32[]{:S(2)}) copy-start(s32[1,1,64]{2,1,0:T(1,128)} %param.15) | copy-start | bytes 772
  56.1 437.5 %all-reduce.7.cloned.1.call-start = ((), (), s32[]{:S(2)}) async-start(), calls=%async_computation.6 | async-start | bytes 262144
  58.2 161.3 %collective-permute-start = (f32[128,64]{0,1:T(8,128)S(1)}, f32[128,64]{0,1:T(8,128)S(1)}, u32[]{:S(2)}, u32[]{:S(2)}) collective-permute-start(f32[128,64]{0,1:T(8,128)S(1)} %constant_dynamic-slice_fusion.4), channel_id=1, source_target_pairs={{32,0},{64,32},{96,64},{128,96},{160,128},{192,160},{224,192},{256... | collective-permute-start | bytes 98312 | tf_op jit(solution)/shard_map/ppermute | solution.py:15
  69.5 153.0 %collective-permute-start.1 = (f32[1]{0:T(128)}, f32[1]{0:T(128)}, u32[]{:S(2)}, u32[]{:S(2)}) collective-permute-start(f32[1]{0:T(128)} %bitcast.13), channel_id=1, source_target_pairs={{480,0},{0,32},{32,64},{64,96},{96,128},{128,160},{160,192},{192,2... | collective-permute-start | bytes 20 | tf_op jit(solution)/shard_map/ppermute | solution.py:15
  72.7 155.1 %copy-start.1 = (f32[1,1,1024,64]{2,3,1,0:T(8,128)S(1)}, f32[1,1,1024,64]{2,3,1,0:T(8,128)}, u32[]{:S(2)}) copy-start(f32[1,1,1024,64]{2,3,1,0:T(8,128)} %param.10) | copy-start | bytes 786436
  219.0 275.7 %copy-start.2 = (f32[1,1,6,1024]{3,1,2,0:T(1,128)S(1)}, f32[1,1,6,1024]{3,1,2,0:T(1,128)}, u32[]{:S(2)}) copy-start(f32[1,1,6,1024]{3,1,2,0:T(1,128)} %param.12) | copy-start | bytes 73732
  219.5 314.7 %copy-start.6 = (f32[1,6,192]{2,0,1:T(1,128)S(1)}, f32[1,6,192]{2,0,1:T(1,128)}, u32[]{:S(2)}) copy-start(f32[1,6,192]{2,0,1:T(1,128)} %param.13) | copy-start | bytes 13828
  219.5 314.8 %copy-start.7 = (f32[1,1,1024]{2,1,0:T(1,128)S(1)}, f32[1,1,1024]{2,1,0:T(1,128)}, u32[]{:S(2)}) copy-start(f32[1,1,1024]{2,1,0:T(1,128)} %param.11) | copy-start | bytes 12292
  219.5 6.9 collective-permute-start.2
  228.3 0.7 copy-start.4
  229.0 514.6 %reduce-scatter.6.cloned.1.call-start = ((), (), s32[]{:S(2)}) async-start(), calls=%async_computation.4 | async-start | bytes 270336 | tf_op jit(solution)/shard_map/reduce_scatter | solution.py:70
  629.2 0.6 copy-start.10
  630.9 433.0 %all-reduce.9.cloned.1.call-start = ((), (), s32[]{:S(2)}) async-start(), calls=%async_computation.7 | async-start | bytes 262144
  632.0 158.2 %collective-permute-start.3 = (f32[128,64]{0,1:T(8,128)S(1)}, f32[128,64]{0,1:T(8,128)S(1)}, u32[]{:S(2)}, u32[]{:S(2)}) collective-permute-start(f32[128,64]{0,1:T(8,128)S(1)} %constant_dynamic-slice_fusion.2), channel_id=1, source_target_pairs={{32,0},{64,32},{96,64},{128,96},{160,128},{192,160},{224,192},{256... | collective-permute-start | bytes 98312 | tf_op jit(solution)/shard_map/ppermute | solution.py:15
  790.3 6.9 collective-permute-start.4
  798.9 0.7 copy-start.5
  799.6 514.7 %reduce-scatter.8.cloned.1.call-start = ((), (), s32[]{:S(2)}) async-start(), calls=%async_computation.5 | async-start | bytes 270336 | tf_op jit(solution)/shard_map/reduce_scatter | solution.py:70
  1202.0 433.0 %all-reduce.11.cloned.1.call-start = ((), (), s32[]{:S(2)}) async-start(), calls=%async_computation.8 | async-start | bytes 262144
  1203.3 158.0 %collective-permute-start.5 = (f32[128,64]{0,1:T(8,128)S(1)}, f32[128,64]{0,1:T(8,128)S(1)}, u32[]{:S(2)}, u32[]{:S(2)}) collective-permute-start(f32[128,64]{0,1:T(8,128)S(1)} %constant_dynamic-slice_fusion), channel_id=1, source_target_pairs={{32,0},{64,32},{96,64},{128,96},{160,128},{192,160},{224,192},{256... | collective-permute-start | bytes 98312 | tf_op jit(solution)/shard_map/ppermute | solution.py:15
  1361.4 6.8 collective-permute-start.6
  1370.0 0.7 copy-start.3
Sparse Core Ops, SparseCore 0:
  56.2 116.5 reduce-scatter.3
  229.1 264.4 all-reduce.6
  631.1 112.4 reduce-scatter.5
  799.7 264.1 all-reduce.8
  1202.2 112.1 reduce-scatter.7
  1370.8 264.1 all-reduce.10
